TPU v7x, 128 devices: a whole 4x4x4 slice. The times are simulated.
128 devices in a mesh: attn: 4 (over x), expert: 32 (over y, z, core).
Axes of the slice: x: 4, y: 4, z: 4, core: 2. Of those that a mesh axis runs over, the one named last changes fastest.
Arguments:
- tokens: bfloat16 [2, 1024, 7168], P(None, ('attn', 'expert')), may hold values from -6 to 6
- routes: int32 [2, 1024, 8], P(None, ('attn', 'expert')), may hold values from 0 to 47, all different within a row; in each aligned block of 8 rows (0 to 7, 8 to 15, ..., all dimensions but the last counted through in order) at most 2 rows name the same one
- route_weights: float32 [2, 1024, 8], P(None, ('attn', 'expert')), may hold values from 0.2 to 1
- slot_expert: int32 [64], replicated, may hold values from 0 to 47, as said below
- w_gate: bfloat16 [64, 7168, 1024], P('expert', None, 'attn'), as said below
- w_up: bfloat16 [64, 7168, 1024], P('expert', None, 'attn'), as said below
- w_down: bfloat16 [64, 1024, 7168], P('expert', 'attn'), as said below
Outputs:
- combined: bfloat16 [2, 1024, 7168], P(None, ('attn', 'expert'))
Inputs may be any that keep to these rules, and one draw needn't show every extreme that they name: `routes`: in each micro-step at most 2 of one device's 8 rows choose the same expert, and some expert reaches 2. `slot_expert`: every expert of the window is held by at least one slot; some are held by several. `w_gate`: slots that hold the same expert hold identical gate projections. `w_up`: slots that hold the same expert hold identical up projections. `w_down`: slots that hold the same expert hold identical down projections.
All inputs are finite; a program needn't handle non-finite values.
Results may differ from a plain program's by a relative error of at most 0.0064.
Values may be sent and summed in bfloat16 or wider, within the bound.
No kernel may reach another device: no remote copies, remote signals or barrier semaphores. Data moves between devices by JAX's collectives and lax.ppermute only.
A program may use at most 128 MiB of HBM per device.

v0:
```python
import jax
import jax.numpy as jnp
from jax import lax
from jax.sharding import PartitionSpec as P

TOP = 8


def place_routes(chosen, slot_expert, replica_rank, slot_ids, earlier):
    matches = chosen[:, None] == slot_expert[None, :]
    replicas = jnp.sum(matches.astype(jnp.int32), axis=1)
    earlier_same = jnp.sum(
        ((chosen[:, None] == chosen[None, :]) & earlier).astype(jnp.int32), axis=1
    )
    replica_pick = earlier_same % replicas
    position = earlier_same // replicas
    selected = matches & (replica_rank[None, :] == replica_pick[:, None])
    target = jnp.sum(jnp.where(selected, slot_ids[None, :], 0), axis=1)
    return (target, position)


def run_quarter(row_block, gate_cols, up_cols, down_rows):
    gate_value = jnp.dot(row_block, gate_cols, preferred_element_type=jnp.float32)
    up_value = jnp.dot(row_block, up_cols, preferred_element_type=jnp.float32)
    hidden = (jax.nn.silu(gate_value) * up_value).astype(jnp.bfloat16)
    return jnp.dot(hidden, down_rows, preferred_element_type=jnp.float32)


def body(tokens, routes, route_weights, slot_expert, w_gate, w_up, w_down):
    groups = lax.axis_size("attn")
    columns = lax.axis_size("expert")
    holders = slot_expert.shape[0]
    per_device = holders // columns
    experts = 3 * holders // 4
    local_rows = tokens.shape[1]
    width = tokens.shape[2]
    capacity = max(2, (local_rows * TOP + experts - 1) // experts)
    route_total = local_rows * TOP
    cells = per_device * columns * capacity
    slot_ids = jnp.arange(holders, dtype=jnp.int32)
    same_holder = slot_expert[:, None] == slot_expert[None, :]
    replica_rank = jnp.sum(
        (same_holder & (slot_ids[None, :] < slot_ids[:, None])).astype(jnp.int32), axis=1
    )
    route_ids = jnp.arange(route_total, dtype=jnp.int32)
    earlier = route_ids[:, None] > route_ids[None, :]
    cell_ids = jnp.arange(cells, dtype=jnp.int32)
    outputs = []
    for micro in range(tokens.shape[0]):
        chosen = routes[micro].reshape(-1)
        token_rows = tokens[micro]
        target, position = place_routes(chosen, slot_expert, replica_rank, slot_ids, earlier)
        flat_cell = (target % per_device * columns + target // per_device) * capacity + position
        hits = (cell_ids[:, None] == flat_cell[None, :]).reshape(cells, local_rows, TOP)
        placing = jnp.any(hits, axis=2).astype(jnp.bfloat16)
        outgoing = jnp.dot(placing, token_rows, preferred_element_type=jnp.float32).astype(
            jnp.bfloat16
        )
        outgoing = outgoing.reshape(per_device, columns, capacity, width)
        copies = jnp.broadcast_to(outgoing[:, None], (per_device, groups, columns, capacity, width))
        copies = copies.reshape(per_device, groups * columns, capacity, width)
        arrived = lax.all_to_all(
            copies, ("attn", "expert"), split_axis=1, concat_axis=1, tiled=True
        )
        partials = []
        for slot_local in range(per_device):
            row_block = arrived[slot_local].reshape(-1, width)
            result = run_quarter(
                row_block, w_gate[slot_local], w_up[slot_local], w_down[slot_local]
            )
            partials.append(result.astype(jnp.bfloat16).reshape(groups, columns, capacity, width))
        partial_value = jnp.stack(partials, axis=0)
        pieces = partial_value.reshape(per_device, groups * columns, capacity, width)
        pieces = lax.all_to_all(pieces, ("attn", "expert"), split_axis=1, concat_axis=1, tiled=True)
        pieces = pieces.reshape(per_device, groups, columns, capacity, width)
        returned = jnp.sum(pieces.astype(jnp.float32), axis=1).astype(jnp.bfloat16)
        returned = returned.reshape(cells, width)
        picked = returned[flat_cell].astype(jnp.float32)
        weights_now = route_weights[micro].reshape(-1)
        blended = jnp.sum((picked * weights_now[:, None]).reshape(local_rows, TOP, width), axis=1)
        outputs.append(blended.astype(jnp.bfloat16))
    return jnp.stack(outputs)


def solution(mesh):
    in_specs = (
        P(None, ("attn", "expert"), None),
        P(None, ("attn", "expert"), None),
        P(None, ("attn", "expert"), None),
        P(),
        P("expert", None, "attn"),
        P("expert", None, "attn"),
        P("expert", "attn", None),
    )
    out_specs = P(None, ("attn", "expert"), None)
    return jax.shard_map(body, mesh=mesh, in_specs=in_specs, out_specs=out_specs, check_vma=False)
```

profile of v0, /device:TPU:23, one launch (start us, length us, event | category | flops | bytes accessed | tf_op | source)
XLA Modules:
  0.0 447.9 jit_solution(13728672464697637354)
XLA Ops:
  0.9 1.0 fusion.94
  2.0 0.9 select_reduce_fusion.1
  3.4 1.6 convolution_convert_fusion.5
  5.0 1.7 broadcast_in_dim.29
  6.7 2.8 copy.22
  9.4 6.2 %broadcast_in_dim.30 = bf16[2,4,32,2,7168]{4,3,0,2,1:T(2,128)(2,1)} broadcast(bf16[2,32,2,7168]{3,2,0,1:T(2,128)(2,1)S(1)} %copy.22), dimensions={0,2,3,4} | broadcast | bytes 9175040 | tf_op jit(solution)/shard_map/broadcast_in_dim | solution.py:60
  15.6 11.0 %all-to-all-start = ((bf16[2,128,2,7168]{3,2,0,1:T(2,128)(2,1)}), bf16[2,128,2,7168]{3,2,0,1:T(2,128)(2,1)}, u32[]{:S(2)}, u32[]{:S(2)}) async-start(bf16[2,128,2,7168]{3,2,0,1:T(2,128)(2,1)} %bitcast.160), calls=%async_computation | async-start | bytes 14680064 | tf_op jit(solution)/shard_map/all_to_all | solution.py:62
  27.7 1.7 broadcast_in_dim.31
  29.4 2.8 copy.26
  32.2 86.8 %all-to-all-done = bf16[2,128,2,7168]{3,2,0,1:T(2,128)(2,1)} async-done(((bf16[2,128,2,7168]{3,2,0,1:T(2,128)(2,1)}), bf16[2,128,2,7168]{3,2,0,1:T(2,128)(2,1)}, u32[]{:S(2)}, u32[]{:S(2)}) %all-to-all-start) | async-done | bytes 7340064 | tf_op jit(solution)/shard_map/all_to_all | solution.py:62
  119.0 6.1 %broadcast_in_dim.32 = bf16[2,4,32,2,7168]{4,3,0,2,1:T(2,128)(2,1)} broadcast(bf16[2,32,2,7168]{3,2,0,1:T(2,128)(2,1)S(1)} %copy.26), dimensions={0,2,3,4} | broadcast | bytes 9175040 | tf_op jit(solution)/shard_map/broadcast_in_dim | solution.py:60
  125.1 7.7 %all-to-all-start.2 = ((bf16[2,128,2,7168]{3,2,0,1:T(2,128)(2,1)}), bf16[2,128,2,7168]{3,2,0,1:T(2,128)(2,1)}, u32[]{:S(2)}, u32[]{:S(2)}) async-start(bf16[2,128,2,7168]{3,2,0,1:T(2,128)(2,1)} %bitcast.161), calls=%async_computation.2 | async-start | bytes 14680064 | tf_op jit(solution)/shard_map/all_to_all | solution.py:62
  132.7 7.7 %fusion.129 = (bf16[1,128,2,7168]{3,2,0,1:T(2,128)(2,1)}, bf16[1,128,2,7168]{3,2,0,1:T(2,128)(2,1)}) fusion(bf16[2,128,2,7168]{3,2,0,1:T(2,128)(2,1)} %all-to-all-done), kind=kLoop, calls=%fused_computation.173 | loop fusion | bytes 14680064 | tf_op jit(solution)/shard_map/slice | solution.py:67
  140.4 8.4 %reshape_squeeze.12 = bf16[256,7168]{1,0:T(8,128)(2,1)} reshape(bf16[1,128,2,7168]{3,2,0,1:T(2,128)(2,1)} %get-tuple-element.18) | data formatting | bytes 7340032 | tf_op jit(solution)/shard_map/reshape;squeeze | solution.py:67
  148.8 4.3 fusion.18
  153.1 10.1 %convolution_convert_fusion.3 = bf16[256,7168]{1,0:T(8,128)(2,1)} fusion(bf16[2,256,7168]{2,1,0:T(8,128)(2,1)} %param.13, bf16[256,7168]{1,0:T(8,128)(2,1)} %reshape_squeeze.12, bf16[2,7168,256]{2,1,0:T(8,128)(2,1)} %param.12, f32[256,256]{1,0:T(8,128)S(1)} %fusion.18), kind=kOutput, calls=%fused_computation.5 | convolution fusion | flops 1881276416 | bytes 14942208 | tf_op jit(solution)/shard_map/dot_general | solution.py:26
  163.2 8.1 %stack.19 = bf16[1,128,2,7168]{3,2,1,0:T(2,128)(2,1)} reshape(bf16[256,7168]{1,0:T(8,128)(2,1)} %convolution_convert_fusion.3) | data formatting | bytes 7340032 | tf_op jit(solution)/shard_map/stack | solution.py:72
  171.3 8.6 %reshape_squeeze.13 = bf16[256,7168]{1,0:T(8,128)(2,1)} reshape(bf16[1,128,2,7168]{3,2,0,1:T(2,128)(2,1)} %get-tuple-element.19) | data formatting | bytes 7340032 | tf_op jit(solution)/shard_map/reshape;squeeze | solution.py:67
  179.9 4.3 fusion.8
  184.2 10.1 %convolution_convert_fusion.2 = bf16[256,7168]{1,0:T(8,128)(2,1)} fusion(bf16[2,256,7168]{2,1,0:T(8,128)(2,1)} %param.13, bf16[256,7168]{1,0:T(8,128)(2,1)} %reshape_squeeze.13, bf16[2,7168,256]{2,1,0:T(8,128)(2,1)} %param.12, f32[256,256]{1,0:T(8,128)S(1)} %fusion.8), kind=kOutput, calls=%fused_computation.4 | convolution fusion | flops 1881276416 | bytes 14942208 | tf_op jit(solution)/shard_map/dot_general | solution.py:26
  194.3 8.1 %stack.20 = bf16[1,128,2,7168]{3,2,1,0:T(2,128)(2,1)} reshape(bf16[256,7168]{1,0:T(8,128)(2,1)} %convolution_convert_fusion.2) | data formatting | bytes 7340032 | tf_op jit(solution)/shard_map/stack | solution.py:72
  202.4 11.8 %pad_maximum_fusion = bf16[2,128,2,7168]{3,2,0,1:T(2,128)(2,1)} fusion(bf16[1,128,2,7168]{3,2,0,1:T(2,128)(2,1)} %bitcast.164, bf16[1,128,2,7168]{3,2,0,1:T(2,128)(2,1)} %bitcast.162), kind=kLoop, calls=%fused_computation.8 | loop fusion | flops 3670016 | bytes 14680064 | tf_op jit(solution)/shard_map/stack | solution.py:72
  214.2 9.1 %all-to-all-done.2 = bf16[2,128,2,7168]{3,2,0,1:T(2,128)(2,1)} async-done(((bf16[2,128,2,7168]{3,2,0,1:T(2,128)(2,1)}), bf16[2,128,2,7168]{3,2,0,1:T(2,128)(2,1)}, u32[]{:S(2)}, u32[]{:S(2)}) %all-to-all-start.2) | async-done | bytes 7340064 | tf_op jit(solution)/shard_map/all_to_all | solution.py:62
  223.4 7.7 %all-to-all-start.1 = ((bf16[2,128,2,7168]{3,2,0,1:T(2,128)(2,1)}), bf16[2,128,2,7168]{3,2,0,1:T(2,128)(2,1)}, u32[]{:S(2)}, u32[]{:S(2)}) async-start(bf16[2,128,2,7168]{3,2,0,1:T(2,128)(2,1)} %pad_maximum_fusion), calls=%async_computation.1 | async-start | bytes 14680064 | tf_op jit(solution)/shard_map/all_to_all | solution.py:74
  231.1 7.7 %fusion.130 = (bf16[1,128,2,7168]{3,2,0,1:T(2,128)(2,1)}, bf16[1,128,2,7168]{3,2,0,1:T(2,128)(2,1)}) fusion(bf16[2,128,2,7168]{3,2,0,1:T(2,128)(2,1)} %all-to-all-done.2), kind=kLoop, calls=%fused_computation.174 | loop fusion | bytes 14680064 | tf_op jit(solution)/shard_map/slice | solution.py:67
  238.8 8.4 %reshape_squeeze.14 = bf16[256,7168]{1,0:T(8,128)(2,1)} reshape(bf16[1,128,2,7168]{3,2,0,1:T(2,128)(2,1)} %get-tuple-element.20) | data formatting | bytes 7340032 | tf_op jit(solution)/shard_map/reshape;squeeze | solution.py:67
  247.2 4.3 fusion.16
  251.5 10.0 %convolution_convert_fusion.1 = bf16[256,7168]{1,0:T(8,128)(2,1)} fusion(bf16[2,256,7168]{2,1,0:T(8,128)(2,1)} %param.13, bf16[256,7168]{1,0:T(8,128)(2,1)} %reshape_squeeze.14, bf16[2,7168,256]{2,1,0:T(8,128)(2,1)} %param.12, f32[256,256]{1,0:T(8,128)S(1)} %fusion.16), kind=kOutput, calls=%fused_computation.3 | convolution fusion | flops 1881276416 | bytes 14942208 | tf_op jit(solution)/shard_map/dot_general | solution.py:26
  261.5 8.1 %stack.22 = bf16[1,128,2,7168]{3,2,1,0:T(2,128)(2,1)} reshape(bf16[256,7168]{1,0:T(8,128)(2,1)} %convolution_convert_fusion.1) | data formatting | bytes 7340032 | tf_op jit(solution)/shard_map/stack | solution.py:72
  269.7 8.8 %reshape_squeeze.15 = bf16[256,7168]{1,0:T(8,128)(2,1)} reshape(bf16[1,128,2,7168]{3,2,0,1:T(2,128)(2,1)} %get-tuple-element.21) | data formatting | bytes 7340032 | tf_op jit(solution)/shard_map/reshape;squeeze | solution.py:67
  278.5 4.3 fusion.6
  282.8 10.0 %convolution_convert_fusion = bf16[256,7168]{1,0:T(8,128)(2,1)} fusion(bf16[2,256,7168]{2,1,0:T(8,128)(2,1)} %param.13, bf16[256,7168]{1,0:T(8,128)(2,1)} %reshape_squeeze.15, bf16[2,7168,256]{2,1,0:T(8,128)(2,1)} %param.12, f32[256,256]{1,0:T(8,128)S(1)} %fusion.6), kind=kOutput, calls=%fused_computation.2 | convolution fusion | flops 1881276416 | bytes 14942208 | tf_op jit(solution)/shard_map/dot_general | solution.py:26
  292.8 8.1 %stack.23 = bf16[1,128,2,7168]{3,2,1,0:T(2,128)(2,1)} reshape(bf16[256,7168]{1,0:T(8,128)(2,1)} %convolution_convert_fusion) | data formatting | bytes 7340032 | tf_op jit(solution)/shard_map/stack | solution.py:72
  300.9 11.8 %pad_maximum_fusion.1 = bf16[2,128,2,7168]{3,2,0,1:T(2,128)(2,1)} fusion(bf16[1,128,2,7168]{3,2,0,1:T(2,128)(2,1)} %bitcast.165, bf16[1,128,2,7168]{3,2,0,1:T(2,128)(2,1)} %bitcast.163), kind=kLoop, calls=%fused_computation.9 | loop fusion | flops 3670016 | bytes 14680064 | tf_op jit(solution)/shard_map/stack | solution.py:72
  312.7 9.0 %all-to-all-done.1 = bf16[2,128,2,7168]{3,2,0,1:T(2,128)(2,1)} async-done(((bf16[2,128,2,7168]{3,2,0,1:T(2,128)(2,1)}), bf16[2,128,2,7168]{3,2,0,1:T(2,128)(2,1)}, u32[]{:S(2)}, u32[]{:S(2)}) %all-to-all-start.1) | async-done | bytes 7340064 | tf_op jit(solution)/shard_map/all_to_all | solution.py:74
  321.7 7.7 %all-to-all-start.3 = ((bf16[2,128,2,7168]{3,2,0,1:T(2,128)(2,1)}), bf16[2,128,2,7168]{3,2,0,1:T(2,128)(2,1)}, u32[]{:S(2)}, u32[]{:S(2)}) async-start(bf16[2,128,2,7168]{3,2,0,1:T(2,128)(2,1)} %pad_maximum_fusion.1), calls=%async_computation.3 | async-start | bytes 14680064 | tf_op jit(solution)/shard_map/all_to_all | solution.py:74
  329.5 10.2 %reduce_sum.118 = bf16[2,32,2,7168]{3,2,0,1:T(2,128)(2,1)S(1)} reduce(bf16[2,4,32,2,7168]{4,3,0,2,1:T(2,128)(2,1)} %bitcast.10, bf16[]{:T(256)} %constant.73.clone.1), dimensions={1}, to_apply=%region_5.6 | reduce | flops 2752512 | bytes 9175042 | tf_op jit(solution)/shard_map/reduce_sum | solution.py:76
  339.6 2.5 copy.25
  342.1 4.1 reshape.497
  346.2 73.9 %all-to-all-done.3 = bf16[2,128,2,7168]{3,2,0,1:T(2,128)(2,1)} async-done(((bf16[2,128,2,7168]{3,2,0,1:T(2,128)(2,1)}), bf16[2,128,2,7168]{3,2,0,1:T(2,128)(2,1)}, u32[]{:S(2)}, u32[]{:S(2)}) %all-to-all-start.3) | async-done | bytes 7340064 | tf_op jit(solution)/shard_map/all_to_all | solution.py:74
  420.0 11.4 %reduce_sum.125 = bf16[2,32,2,7168]{3,2,0,1:T(2,128)(2,1)} reduce(bf16[2,4,32,2,7168]{4,3,0,2,1:T(2,128)(2,1)} %bitcast.22, bf16[]{:T(256)} %constant.73.clone.1), dimensions={1}, to_apply=%region_11.12 | reduce | flops 2752512 | bytes 9175042 | tf_op jit(solution)/shard_map/reduce_sum | solution.py:76
  431.5 4.0 copy.29
  435.4 5.1 %reshape.500 = bf16[128,7168]{1,0:T(8,128)(2,1)} reshape(bf16[2,32,2,7168]{3,2,1,0:T(2,128)(2,1)} %copy.29) | data formatting | bytes 3670016 | tf_op jit(solution)/shard_map/reshape | solution.py:77
  440.6 1.1 gather_fusion
  441.7 0.8 fusion.33
  442.5 3.7 gather_fusion.1
  446.2 0.8 fusion.32
  447.0 0.7 pad_maximum_fusion.2
  (24 shorter events, 2.7 us)
Async XLA Ops:
  15.6 11.5 %copy-start = (bf16[2,8,7168]{2,1,0:T(8,128)(2,1)S(1)}, bf16[2,8,7168]{2,1,0:T(8,128)(2,1)}, u32[]{:S(2)}) copy-start(bf16[2,8,7168]{2,1,0:T(8,128)(2,1)} %param.7) | copy-start | bytes 688132
  15.6 103.4 %all-to-all-start = ((bf16[2,128,2,7168]{3,2,0,1:T(2,128)(2,1)}), bf16[2,128,2,7168]{3,2,0,1:T(2,128)(2,1)}, u32[]{:S(2)}, u32[]{:S(2)}) async-start(bf16[2,128,2,7168]{3,2,0,1:T(2,128)(2,1)} %bitcast.160), calls=%async_computation | async-start | bytes 14680064 | tf_op jit(solution)/shard_map/all_to_all | solution.py:62
  125.1 98.3 %all-to-all-start.2 = ((bf16[2,128,2,7168]{3,2,0,1:T(2,128)(2,1)}), bf16[2,128,2,7168]{3,2,0,1:T(2,128)(2,1)}, u32[]{:S(2)}, u32[]{:S(2)}) async-start(bf16[2,128,2,7168]{3,2,0,1:T(2,128)(2,1)} %bitcast.161), calls=%async_computation.2 | async-start | bytes 14680064 | tf_op jit(solution)/shard_map/all_to_all | solution.py:62
  223.4 98.4 %all-to-all-start.1 = ((bf16[2,128,2,7168]{3,2,0,1:T(2,128)(2,1)}), bf16[2,128,2,7168]{3,2,0,1:T(2,128)(2,1)}, u32[]{:S(2)}, u32[]{:S(2)}) async-start(bf16[2,128,2,7168]{3,2,0,1:T(2,128)(2,1)} %pad_maximum_fusion), calls=%async_computation.1 | async-start | bytes 14680064 | tf_op jit(solution)/shard_map/all_to_all | solution.py:74
  312.7 16.7 %copy-start.1 = (f32[2,8,8]{2,1,0:T(8,128)S(1)}, f32[2,8,8]{2,1,0:T(8,128)}, u32[]{:S(2)}) copy-start(f32[2,8,8]{2,1,0:T(8,128)} %param.9) | copy-start | bytes 1540
  321.7 98.3 %all-to-all-start.3 = ((bf16[2,128,2,7168]{3,2,0,1:T(2,128)(2,1)}), bf16[2,128,2,7168]{3,2,0,1:T(2,128)(2,1)}, u32[]{:S(2)}, u32[]{:S(2)}) async-start(bf16[2,128,2,7168]{3,2,0,1:T(2,128)(2,1)} %pad_maximum_fusion.1), calls=%async_computation.3 | async-start | bytes 14680064 | tf_op jit(solution)/shard_map/all_to_all | solution.py:74
where the time goes:
time: 455 us; the launch traced here: 448 us
  waiting for transfers between devices  179 us (39%)
  local copies, waits for them, and re-layouts  125 us (27%)
  matrix products  59.6 us (13%)
  other arithmetic  49.9 us (11%)
  starting transfers between devices  34 us (7%)
    all_to_all x2, waiting for transfers between devices, body(): lax.all_to_all(copies, ('attn', 'expert'), split_axis=1, concat_axis=1, t...  96 us
    all_to_all x2, waiting for transfers between devices, body(): lax.all_to_all(pieces, ('attn', 'expert'), split_axis=1, concat_axis=1, t...  82.9 us
    dot_general x4, matrix products, run_quarter(): return jnp.dot(hidden, down_rows, preferred_element_type=jnp.float32)  40.3 us
    another operation x4, local copies, waits for them, and re-layouts, body(): row_block = arrived[slot_local].reshape(-1, width)  34.2 us
    another operation x4, local copies, waits for them, and re-layouts, body(): partial_value = jnp.stack(partials, axis=0)  32.5 us
    another operation x2, other arithmetic, body(): partial_value = jnp.stack(partials, axis=0)  23.6 us
    reduce_sum x2, other arithmetic, body(): returned = jnp.sum(pieces.astype(jnp.float32), axis=1).astype(jnp.bfloat16)  21.6 us
    broadcast_in_dim x6, local copies, waits for them, and re-layouts, body(): jnp.broadcast_to(outgoing[:, None], (per_device, groups, columns, capacit...  21.1 us
  transfers between devices with their start and end apart: 4, of which 4 were waited for; matrix products, arithmetic and copies ran while one was open for 41% of the time, Pallas kernels for 0%

commit v1 on v0

--- a/solution.py
+++ b/solution.py
@@ -71,7 +71,15 @@
             partials.append(result.astype(jnp.bfloat16).reshape(groups, columns, capacity, width))
         partial_value = jnp.stack(partials, axis=0)
         pieces = partial_value.reshape(per_device, groups * columns, capacity, width)
-        pieces = lax.all_to_all(pieces, ("attn", "expert"), split_axis=1, concat_axis=1, tiled=True)
+        pieces = jnp.concatenate(
+            lax.all_to_all(
+                jnp.stack(jnp.split(pieces, lax.axis_size(("attn", "expert")), axis=1)),
+                ("attn", "expert"),
+                0,
+                0,
+            ),
+            axis=1,
+        )
         pieces = pieces.reshape(per_device, groups, columns, capacity, width)
         returned = jnp.sum(pieces.astype(jnp.float32), axis=1).astype(jnp.bfloat16)
         returned = returned.reshape(cells, width)

time: 455 us -> 722 us (1.59); the launches traced: 448 us -> 707 us
  local copies, waits for them, and re-layouts: 125 us -> 419 us
  other arithmetic: 49.9 us -> 26.4 us
  waiting for transfers between devices: 179 us -> 162 us
    unnamed x4 -> x262, local copies, waits for them, and re-layouts: 0.01 us -> 282 us
    another operation x2 -> x0, other arithmetic: 23.6 us -> none  [body(): partial_value = jnp.stack(partials, axis=0)]
    another operation x4 -> x6, local copies, waits for them, and re-layouts: 32.5 us -> 41.8 us  [body(): partial_value = jnp.stack(partials, axis=0)]
    all_to_all x2, waiting for transfers between devices: 96 us -> 86.8 us  [body(): lax.all_to_all(copies, ('attn', 'expert'), split_axis=1, concat_axis=1, t...]
    all_to_all x2, waiting for transfers between devices: 82.9 us -> 75.6 us  [body(): lax.all_to_all(jnp.stack(jnp.split(pieces, lax.axis_size(('attn', 'expert...]
  transfers between devices with their start and end apart: 4 -> 4, of which waited for: 4 -> 2; matrix products, arithmetic and copies ran while one was open for 41% -> 64% of each run, Pallas kernels for 0% -> 0%
where the time goes in v1:
time: 722 us; the launch traced here: 707 us
  local copies, waits for them, and re-layouts  419 us (58%)
  waiting for transfers between devices  162 us (22%)
  matrix products  59.5 us (8%)
  starting transfers between devices  39.9 us (6%)
  other arithmetic  26.4 us (4%)
    unnamed x262, local copies, waits for them, and re-layouts  282 us
    all_to_all x2, waiting for transfers between devices, body(): lax.all_to_all(copies, ('attn', 'expert'), split_axis=1, concat_axis=1, t...  86.8 us
    all_to_all x2, waiting for transfers between devices, body(): lax.all_to_all(jnp.stack(jnp.split(pieces, lax.axis_size(('attn', 'expert...  75.6 us
    another operation x6, local copies, waits for them, and re-layouts, body(): partial_value = jnp.stack(partials, axis=0)  41.8 us
    dot_general x4, matrix products, run_quarter(): return jnp.dot(hidden, down_rows, preferred_element_type=jnp.float32)  40.1 us
    another operation x4, local copies, waits for them, and re-layouts, body(): row_block = arrived[slot_local].reshape(-1, width)  33.8 us
    reduce_sum x2, other arithmetic, body(): returned = jnp.sum(pieces.astype(jnp.float32), axis=1).astype(jnp.bfloat16)  21.6 us
    broadcast_in_dim x6, local copies, waits for them, and re-layouts, body(): jnp.broadcast_to(outgoing[:, None], (per_device, groups, columns, capacit...  21.1 us
  transfers between devices with their start and end apart: 4, of which 2 were waited for; matrix products, arithmetic and copies ran while one was open for 64% of the time, Pallas kernels for 0%

profile of v1, /device:TPU:23, one launch (start us, length us, event | category | flops | bytes accessed | tf_op | source)
XLA Modules:
  0.0 707.5 jit_solution(4725369940107437729)
XLA Ops:
  3.4 1.6 convolution_convert_fusion.5
  5.0 1.7 broadcast_in_dim.29
  6.7 2.8 copy.520
  9.4 6.2 broadcast_in_dim.30
  15.6 11.0 %all-to-all-start = ((bf16[2,128,2,7168]{3,2,0,1:T(2,128)(2,1)}), bf16[2,128,2,7168]{3,2,0,1:T(2,128)(2,1)}, u32[]{:S(2)}, u32[]{:S(2)}) async-start(bf16[2,128,2,7168]{3,2,0,1:T(2,128)(2,1)} %bitcast.1693), calls=%async_computation | async-start | bytes 14680064 | tf_op jit(solution)/shard_map/all_to_all | solution.py:62
  27.7 1.7 broadcast_in_dim.31
  29.5 2.8 copy.649
  32.2 86.8 %all-to-all-done = bf16[2,128,2,7168]{3,2,0,1:T(2,128)(2,1)} async-done(((bf16[2,128,2,7168]{3,2,0,1:T(2,128)(2,1)}), bf16[2,128,2,7168]{3,2,0,1:T(2,128)(2,1)}, u32[]{:S(2)}, u32[]{:S(2)}) %all-to-all-start) | async-done | bytes 7340064 | tf_op jit(solution)/shard_map/all_to_all | solution.py:62
  119.0 6.0 broadcast_in_dim.32
  125.1 8.0 %all-to-all-start.2 = ((bf16[2,128,2,7168]{3,2,0,1:T(2,128)(2,1)}), bf16[2,128,2,7168]{3,2,0,1:T(2,128)(2,1)}, u32[]{:S(2)}, u32[]{:S(2)}) async-start(bf16[2,128,2,7168]{3,2,0,1:T(2,128)(2,1)} %bitcast.1692), calls=%async_computation.2 | async-start | bytes 14680064 | tf_op jit(solution)/shard_map/all_to_all | solution.py:62
  133.1 7.7 %fusion.129 = (bf16[1,128,2,7168]{3,2,0,1:T(2,128)(2,1)}, bf16[1,128,2,7168]{3,2,0,1:T(2,128)(2,1)}) fusion(bf16[2,128,2,7168]{3,2,0,1:T(2,128)(2,1)} %all-to-all-done), kind=kLoop, calls=%fused_computation.687 | loop fusion | bytes 14680064 | tf_op jit(solution)/shard_map/slice | solution.py:67
  140.8 8.4 %reshape_squeeze.12 = bf16[256,7168]{1,0:T(8,128)(2,1)} reshape(bf16[1,128,2,7168]{3,2,0,1:T(2,128)(2,1)} %get-tuple-element.19) | data formatting | bytes 7340032 | tf_op jit(solution)/shard_map/reshape;squeeze | solution.py:67
  149.2 4.3 fusion.18
  153.5 10.1 %convolution_convert_fusion.3 = bf16[256,7168]{1,0:T(8,128)(2,1)} fusion(bf16[2,256,7168]{2,1,0:T(8,128)(2,1)} %param.13, bf16[256,7168]{1,0:T(8,128)(2,1)} %reshape_squeeze.12, bf16[2,7168,256]{2,1,0:T(8,128)(2,1)} %param.12, f32[256,256]{1,0:T(8,128)S(1)} %fusion.18), kind=kOutput, calls=%fused_computation.5 | convolution fusion | flops 1881276416 | bytes 14942208 | tf_op jit(solution)/shard_map/dot_general | solution.py:26
  163.5 8.1 %stack.793 = bf16[1,128,2,7168]{3,2,1,0:T(2,128)(2,1)} reshape(bf16[256,7168]{1,0:T(8,128)(2,1)} %convolution_convert_fusion.3) | data formatting | bytes 7340032 | tf_op jit(solution)/shard_map/stack | solution.py:72
  171.7 6.3 constant_dynamic-update-slice_fusion.1
  178.0 8.6 %reshape_squeeze.13 = bf16[256,7168]{1,0:T(8,128)(2,1)} reshape(bf16[1,128,2,7168]{3,2,0,1:T(2,128)(2,1)} %get-tuple-element.18) | data formatting | bytes 7340032 | tf_op jit(solution)/shard_map/reshape;squeeze | solution.py:67
  186.6 4.3 fusion.8
  190.8 10.0 %convolution_convert_fusion.2 = bf16[256,7168]{1,0:T(8,128)(2,1)} fusion(bf16[2,256,7168]{2,1,0:T(8,128)(2,1)} %param.13, bf16[256,7168]{1,0:T(8,128)(2,1)} %reshape_squeeze.13, bf16[2,7168,256]{2,1,0:T(8,128)(2,1)} %param.12, f32[256,256]{1,0:T(8,128)S(1)} %fusion.8), kind=kOutput, calls=%fused_computation.4 | convolution fusion | flops 1881276416 | bytes 14942208 | tf_op jit(solution)/shard_map/dot_general | solution.py:26
  200.9 8.1 %stack.794 = bf16[1,128,2,7168]{3,2,1,0:T(2,128)(2,1)} reshape(bf16[256,7168]{1,0:T(8,128)(2,1)} %convolution_convert_fusion.2) | data formatting | bytes 7340032 | tf_op jit(solution)/shard_map/stack | solution.py:72
  209.0 6.4 constant_dynamic-update-slice_fusion
  230.1 1.5 constant_dynamic-update-slice_fusion.119
  253.8 1.5 constant_dynamic-update-slice_fusion.103
  293.7 1.5 constant_dynamic-update-slice_fusion.76
  295.2 1.5 constant_dynamic-update-slice_fusion.75
  366.1 1.5 constant_dynamic-update-slice_fusion.27
  401.6 1.5 constant_dynamic-update-slice_fusion.3
  404.6 10.7 %all-to-all-start.1 = ((bf16[128,2,1,2,7168]{4,3,1,2,0:T(2,128)(2,1)}), bf16[128,2,1,2,7168]{4,3,1,2,0:T(2,128)(2,1)}, u32[]{:S(2)}, u32[]{:S(2)}) async-start(bf16[128,2,1,2,7168]{4,3,1,2,0:T(2,128)(2,1)} %constant_dynamic-update-slice_fusion.2), calls=%async_computation.1 | async-start | bytes 14680064 | tf_op jit(solution)/shard_map/all_to_all | solution.py:75
  415.3 7.7 %fusion.130 = (bf16[1,128,2,7168]{3,2,0,1:T(2,128)(2,1)}, bf16[1,128,2,7168]{3,2,0,1:T(2,128)(2,1)}) fusion(bf16[2,128,2,7168]{3,2,0,1:T(2,128)(2,1)} %all-to-all-done.2), kind=kLoop, calls=%fused_computation.688 | loop fusion | bytes 14680064 | tf_op jit(solution)/shard_map/slice | solution.py:67
  423.1 8.4 %reshape_squeeze.15 = bf16[256,7168]{1,0:T(8,128)(2,1)} reshape(bf16[1,128,2,7168]{3,2,0,1:T(2,128)(2,1)} %get-tuple-element.20) | data formatting | bytes 7340032 | tf_op jit(solution)/shard_map/reshape;squeeze | solution.py:67
  431.5 4.3 fusion.6
  435.7 10.0 %convolution_convert_fusion = bf16[256,7168]{1,0:T(8,128)(2,1)} fusion(bf16[2,256,7168]{2,1,0:T(8,128)(2,1)} %param.13, bf16[256,7168]{1,0:T(8,128)(2,1)} %reshape_squeeze.15, bf16[2,7168,256]{2,1,0:T(8,128)(2,1)} %param.12, f32[256,256]{1,0:T(8,128)S(1)} %fusion.6), kind=kOutput, calls=%fused_computation.2 | convolution fusion | flops 1881276416 | bytes 14942208 | tf_op jit(solution)/shard_map/dot_general | solution.py:26
  445.8 8.1 %stack.926 = bf16[1,128,2,7168]{3,2,1,0:T(2,128)(2,1)} reshape(bf16[256,7168]{1,0:T(8,128)(2,1)} %convolution_convert_fusion) | data formatting | bytes 7340032 | tf_op jit(solution)/shard_map/stack | solution.py:72
  453.9 8.4 %reshape_squeeze.14 = bf16[256,7168]{1,0:T(8,128)(2,1)} reshape(bf16[1,128,2,7168]{3,2,0,1:T(2,128)(2,1)} %get-tuple-element.21) | data formatting | bytes 7340032 | tf_op jit(solution)/shard_map/reshape;squeeze | solution.py:67
  462.3 4.3 fusion.16
  466.6 10.0 %convolution_convert_fusion.1 = bf16[256,7168]{1,0:T(8,128)(2,1)} fusion(bf16[2,256,7168]{2,1,0:T(8,128)(2,1)} %param.13, bf16[256,7168]{1,0:T(8,128)(2,1)} %reshape_squeeze.14, bf16[2,7168,256]{2,1,0:T(8,128)(2,1)} %param.12, f32[256,256]{1,0:T(8,128)S(1)} %fusion.16), kind=kOutput, calls=%fused_computation.3 | convolution fusion | flops 1881276416 | bytes 14942208 | tf_op jit(solution)/shard_map/dot_general | solution.py:26
  476.6 8.3 %stack.925 = bf16[1,128,2,7168]{3,2,1,0:T(2,128)(2,1)} reshape(bf16[256,7168]{1,0:T(8,128)(2,1)} %convolution_convert_fusion.1) | data formatting | bytes 7340032 | tf_op jit(solution)/shard_map/stack | solution.py:72
  484.9 4.7 constant_dynamic-update-slice_fusion.131
  489.6 2.7 constant_dynamic-update-slice_fusion.130
  576.9 10.2 %all-to-all-start.3 = ((bf16[128,2,1,2,7168]{4,3,1,2,0:T(2,128)(2,1)}), bf16[128,2,1,2,7168]{4,3,1,2,0:T(2,128)(2,1)}, u32[]{:S(2)}, u32[]{:S(2)}) async-start(bf16[128,2,1,2,7168]{4,3,1,2,0:T(2,128)(2,1)} %constant_dynamic-update-slice_fusion.132), calls=%async_computation.3 | async-start | bytes 14680064 | tf_op jit(solution)/shard_map/all_to_all | solution.py:75
  587.1 10.2 %reduce_sum.118 = bf16[2,32,2,7168]{3,2,0,1:T(2,128)(2,1)S(1)} reduce(bf16[2,4,32,2,7168]{4,3,0,2,1:T(2,128)(2,1)} %bitcast.137, bf16[]{:T(256)} %constant.73.clone.1), dimensions={1}, to_apply=%region_5.6 | reduce | flops 2752512 | bytes 9175042 | tf_op jit(solution)/shard_map/reduce_sum | solution.py:84
  597.3 2.6 copy.648
  599.8 4.1 reshape.497
  603.9 75.6 %all-to-all-done.3 = bf16[128,2,1,2,7168]{4,3,1,2,0:T(2,128)(2,1)} async-done(((bf16[128,2,1,2,7168]{4,3,1,2,0:T(2,128)(2,1)}), bf16[128,2,1,2,7168]{4,3,1,2,0:T(2,128)(2,1)}, u32[]{:S(2)}, u32[]{:S(2)}) %all-to-all-start.3) | async-done | bytes 7340064 | tf_op jit(solution)/shard_map/all_to_all | solution.py:75
  679.5 11.5 %reduce_sum.125 = bf16[2,32,2,7168]{3,2,0,1:T(2,128)(2,1)} reduce(bf16[2,4,32,2,7168]{4,3,0,2,1:T(2,128)(2,1)} %bitcast.276, bf16[]{:T(256)} %constant.73.clone.1), dimensions={1}, to_apply=%region_11.12 | reduce | flops 2752512 | bytes 9175042 | tf_op jit(solution)/shard_map/reduce_sum | solution.py:84
  691.0 4.0 copy.777
  695.0 5.1 reshape.500
  702.0 3.7 gather_fusion.1
  (284 shorter events, 272.5 us)
Async XLA Ops:
  15.6 11.5 %copy-start.1 = (bf16[2,8,7168]{2,1,0:T(8,128)(2,1)S(1)}, bf16[2,8,7168]{2,1,0:T(8,128)(2,1)}, u32[]{:S(2)}) copy-start(bf16[2,8,7168]{2,1,0:T(8,128)(2,1)} %param.7) | copy-start | bytes 688132
  15.6 103.4 %all-to-all-start = ((bf16[2,128,2,7168]{3,2,0,1:T(2,128)(2,1)}), bf16[2,128,2,7168]{3,2,0,1:T(2,128)(2,1)}, u32[]{:S(2)}, u32[]{:S(2)}) async-start(bf16[2,128,2,7168]{3,2,0,1:T(2,128)(2,1)} %bitcast.1693), calls=%async_computation | async-start | bytes 14680064 | tf_op jit(solution)/shard_map/all_to_all | solution.py:62
  125.1 279.5 %all-to-all-start.2 = ((bf16[2,128,2,7168]{3,2,0,1:T(2,128)(2,1)}), bf16[2,128,2,7168]{3,2,0,1:T(2,128)(2,1)}, u32[]{:S(2)}, u32[]{:S(2)}) async-start(bf16[2,128,2,7168]{3,2,0,1:T(2,128)(2,1)} %bitcast.1692), calls=%async_computation.2 | async-start | bytes 14680064 | tf_op jit(solution)/shard_map/all_to_all | solution.py:62
  404.6 172.3 %all-to-all-start.1 = ((bf16[128,2,1,2,7168]{4,3,1,2,0:T(2,128)(2,1)}), bf16[128,2,1,2,7168]{4,3,1,2,0:T(2,128)(2,1)}, u32[]{:S(2)}, u32[]{:S(2)}) async-start(bf16[128,2,1,2,7168]{4,3,1,2,0:T(2,128)(2,1)} %constant_dynamic-update-slice_fusion.2), calls=%async_computation.1 | async-start | bytes 14680064 | tf_op jit(solution)/shard_map/all_to_all | solution.py:75
  484.9 4.7 copy-start
  576.9 10.2 %copy-start.2 = (f32[2,8,8]{2,1,0:T(8,128)S(1)}, f32[2,8,8]{2,1,0:T(8,128)}, u32[]{:S(2)}) copy-start(f32[2,8,8]{2,1,0:T(8,128)} %param.9) | copy-start | bytes 1540
  576.9 102.6 %all-to-all-start.3 = ((bf16[128,2,1,2,7168]{4,3,1,2,0:T(2,128)(2,1)}), bf16[128,2,1,2,7168]{4,3,1,2,0:T(2,128)(2,1)}, u32[]{:S(2)}, u32[]{:S(2)}) async-start(bf16[128,2,1,2,7168]{4,3,1,2,0:T(2,128)(2,1)} %constant_dynamic-update-slice_fusion.132), calls=%async_computation.3 | async-start | bytes 14680064 | tf_op jit(solution)/shard_map/all_to_all | solution.py:75
